TPU v7x, 32 devices: a whole 2x2x4 slice. The times are simulated.
32 devices in a mesh: enc: 2 (over core), dp: 4 (over z), mp: 4 (over y, x).
Axes of the slice: x: 2, y: 2, z: 4, core: 2. Of those that a mesh axis runs over, the one named last changes fastest.
Arguments:
- token_ids: int32 [2, 16, 256], P('enc', 'dp'), may hold values from 0 to 30719
- query_lengths: int32 [32], P('dp'), may hold values from 1 to 128, 2048 in all
- negative_mask: int32 [32, 16], replicated, may hold values 0 or 1
- positive_index: int32 [32], replicated, may hold values from 0 to 15
- used_rows: int32 [32], replicated, may hold values 0 or 1
- step_count: int32 [1], replicated, may hold values from 2 to 20
- table: float32 [2, 30720, 768], P('enc', ('dp', 'mp')), may hold values from -0.18 to 0.18
- w_mixed: float32 [2, 768, 3, 768], P('enc', 'dp', None, 'mp'), may hold values from -0.21875 to 0.21875
- w_out: float32 [2, 768, 768], P('enc', 'mp', 'dp'), may hold values from -0.875 to 0.875
- w_inner: float32 [2, 768, 3072], P('enc', 'dp', 'mp'), may hold values from -0.21875 to 0.21875
- w_outer: float32 [2, 3072, 768], P('enc', 'mp', 'dp'), may hold values from -0.109375 to 0.109375
- norm_params: float32 [2, 6, 768], P('enc'), as said below
- table_m: float32 [2, 30720, 768], P('enc', ('dp', 'mp')), may hold values from -1.1234977e-06 to 1.1234977e-06
- table_v: float32 [2, 30720, 768], P('enc', ('dp', 'mp')), may hold values from 6.5198705e-15 to 2.6079482e-14
- mixed_m: float32 [2, 768, 3, 768], P('enc', 'dp', None, 'mp'), may hold values from -1.1234977e-06 to 1.1234977e-06
- mixed_v: float32 [2, 768, 3, 768], P('enc', 'dp', None, 'mp'), may hold values from 6.5198705e-15 to 2.6079482e-14
- out_m: float32 [2, 768, 768], P('enc', 'mp', 'dp'), may hold values from -1.1234977e-06 to 1.1234977e-06
- out_v: float32 [2, 768, 768], P('enc', 'mp', 'dp'), may hold values from 6.5198705e-15 to 2.6079482e-14
- inner_m: float32 [2, 768, 3072], P('enc', 'dp', 'mp'), may hold values from -1.1234977e-06 to 1.1234977e-06
- inner_v: float32 [2, 768, 3072], P('enc', 'dp', 'mp'), may hold values from 6.5198705e-15 to 2.6079482e-14
- outer_m: float32 [2, 3072, 768], P('enc', 'mp', 'dp'), may hold values from -1.1234977e-06 to 1.1234977e-06
- outer_v: float32 [2, 3072, 768], P('enc', 'mp', 'dp'), may hold values from 6.5198705e-15 to 2.6079482e-14
- norms_m: float32 [2, 6, 768], P('enc'), may hold values from -4.4684566e-06 to 4.4684566e-06
- norms_v: float32 [2, 6, 768], P('enc'), may hold values from 1.0431793e-13 to 4.172717e-13
Outputs:
- loss: float32 [], replicated
- grad_norm: float32 [], replicated
- table_new: float32 [2, 30720, 768], P('enc', ('dp', 'mp'))
- table_m_new: float32 [2, 30720, 768], P('enc', ('dp', 'mp'))
- table_v_new: float32 [2, 30720, 768], P('enc', ('dp', 'mp'))
- mixed_new: float32 [2, 768, 3, 768], P('enc', 'dp', None, 'mp')
- mixed_m_new: float32 [2, 768, 3, 768], P('enc', 'dp', None, 'mp')
- mixed_v_new: float32 [2, 768, 3, 768], P('enc', 'dp', None, 'mp')
- out_new: float32 [2, 768, 768], P('enc', 'mp', 'dp')
- out_m_new: float32 [2, 768, 768], P('enc', 'mp', 'dp')
- output_second_moment_next: float32 [2, 768, 768], P('enc', 'mp', 'dp')
- inner_new: float32 [2, 768, 3072], P('enc', 'dp', 'mp')
- inner_m_new: float32 [2, 768, 3072], P('enc', 'dp', 'mp')
- inner_v_new: float32 [2, 768, 3072], P('enc', 'dp', 'mp')
- outer_new: float32 [2, 3072, 768], P('enc', 'mp', 'dp')
- outer_m_new: float32 [2, 3072, 768], P('enc', 'mp', 'dp')
- outer_v_new: float32 [2, 3072, 768], P('enc', 'mp', 'dp')
- norms_new: float32 [2, 6, 768], P('enc')
- norms_m_new: float32 [2, 6, 768], P('enc')
- norms_v_new: float32 [2, 6, 768], P('enc')
Inputs may be any that keep to these rules, and one draw needn't show every extreme that they name: `norm_params`: gains (rows 0, 2, 4) lie in 0.7 to 1.3, shifts (rows 1, 3, 5) are small.
All inputs are finite; a program needn't handle non-finite values. No bound on the sum of `query_lengths` on one device may be relied on, other than what follows from the above.
Results may differ from a plain program's by a relative error of at most 0.015.
Values may be sent and summed in bfloat16 or wider, within the bound.
A program may use at most 192 MiB of HBM per device.

v0:
```python
from functools import partial
import jax
import jax.numpy as jnp
from jax import lax
from jax.sharding import PartitionSpec as P

HEAD = 64
QSLOT = 128
F32 = jnp.float32
BF16 = jnp.bfloat16
exact_arithmetic_level = lax.Precision.HIGHEST
eps_norm = 1e-06
logit_divisor = 0.05
clip_limit = 0.02
beta_one = 0.9
beta_two = 0.999
adam_eps = 1e-08


def layer_norm(x, gain, shift):
    centred = x - jnp.mean(x, -1, keepdims=True)
    spread = jnp.mean(centred * centred, -1, keepdims=True)
    return centred * lax.rsqrt(spread + eps_norm) * gain + shift


def mul(spec, a, b):
    return jnp.einsum(spec, a, b, preferred_element_type=F32)


def token_counts(ids, lens, is_query, base, rows):
    pos = jnp.arange(ids.shape[1])
    slot = pos // QSLOT
    limit = jnp.where(slot[None, :] == 0, lens[:, 0:1], lens[:, 1:2])
    within = (pos % QSLOT)[None, :] < limit
    same = slot[None, :] == jnp.arange(2)[:, None]
    allowed = jnp.where(is_query, same[:, None, :] & within[None], True)
    local = ids - base
    n_hi = -(-rows // 128)
    high = local[..., None] >> 7 == jnp.arange(n_hi)
    low = local[..., None] & 127 == jnp.arange(128)
    left = (allowed[..., None] & high[None]).astype(BF16)
    counts = mul("sbth,btl->sbhl", left, low.astype(BF16))
    return counts.reshape(2 * ids.shape[0], n_hi * 128)[:, :rows]


def contrast(queries, passages, negative_mask, positive_index, used_rows):
    question_direction_rows = queries * lax.rsqrt(
        jnp.sum(queries * queries, -1, keepdims=True) + eps_norm
    )
    document_direction_rows = passages * lax.rsqrt(
        jnp.sum(passages * passages, -1, keepdims=True) + eps_norm
    )
    pairwise_cosine_table = (
        jnp.dot(
            question_direction_rows, document_direction_rows.T, precision=exact_arithmetic_level
        )
        / logit_divisor
    )
    is_positive = jnp.arange(passages.shape[0])[None, :] == positive_index[:, None]
    excluded = (negative_mask == 1) & ~is_positive
    pairwise_cosine_table = jnp.where(excluded, -1e30, pairwise_cosine_table)
    top = jnp.max(pairwise_cosine_table, -1, keepdims=True)
    log_total = top[:, 0] + jnp.log(jnp.sum(jnp.exp(pairwise_cosine_table - top), -1))
    target = jnp.sum(jnp.where(is_positive, pairwise_cosine_table, 0.0), -1)
    weight = used_rows.astype(F32)
    return jnp.sum(weight * (log_total - target)) / jnp.maximum(jnp.sum(weight), 1.0)


def adam_step(weight, grad, first, second, rate, decay, count):
    first_new = beta_one * first + (1.0 - beta_one) * grad
    second_new = beta_two * second + (1.0 - beta_two) * grad * grad
    fix_one = 1.0 - jnp.power(beta_one, count)
    correction_second = 1.0 - jnp.power(beta_two, count)
    update = (
        first_new / fix_one / (jnp.sqrt(second_new / correction_second) + adam_eps) + decay * weight
    )
    return (weight - rate * update, first_new, second_new)


def slot_major(x):
    return x.reshape((x.shape[0] // 2, 2) + x.shape[1:]).swapaxes(0, 1).reshape(x.shape)


def gradients(
    token_ids,
    query_lengths,
    negative_mask,
    positive_index,
    used_rows,
    table,
    w_mixed,
    w_out,
    w_inner,
    w_outer,
    norm_params,
):
    is_query = lax.axis_index("enc") == 0
    d, m = (lax.axis_index("dp"), lax.axis_index("mp"))
    n_mp = lax.axis_size("mp")
    rows, width = (table.shape[1], w_mixed.shape[1])
    hm = w_out.shape[1] // HEAD
    scale = HEAD ** (-0.5)
    norms = norm_params[0]
    base = (d * n_mp + m) * rows
    ids = lax.all_gather(token_ids[0], "dp", axis=0, tiled=True)
    lens = lax.all_gather(query_lengths, "dp", axis=0, tiled=True).reshape(-1, 2)
    blocks = ids.shape[0]
    counts = token_counts(ids, lens, is_query, base, rows)
    cls_ids = jnp.concatenate([ids[:, 0], ids[:, QSLOT]]) - base
    cls_hot = cls_ids[:, None] == jnp.arange(rows)[None, :]

    def mine(x):
        return lax.dynamic_slice_in_dim(x, d * width, width, 1)

    wq, wk, wv = (w_mixed[0, :, i].astype(BF16).reshape(width, hm, HEAD) for i in range(3))
    wo = w_out[0].astype(BF16).reshape(hm, HEAD, width)
    wi, wt = (w_inner[0].astype(BF16), w_outer[0].astype(BF16))
    embedded = lax.reduce_precision(table[0], 8, 7)
    hidden, hidden_back = jax.vjp(layer_norm, embedded, norms[0], norms[1])
    hid = hidden.astype(BF16)
    first_rows = lax.psum(
        jnp.dot(cls_hot.astype(F32), hidden, precision=exact_arithmetic_level), ("dp", "mp")
    )
    first_mine = mine(first_rows).astype(BF16)
    q = lax.psum(mul("ci,ihk->hck", first_mine, wq), "dp").astype(BF16)
    u = mul("hck,ihk->hci", q, wk).astype(BF16)
    u = lax.all_gather(lax.all_gather(u, "dp", axis=2, tiled=True), "mp", axis=0, tiled=True)
    scores = jnp.where(counts[None] > 0, mul("hci,vi->hcv", u, hid) * scale, -1e30)
    top = lax.pmax(jnp.max(scores, -1, keepdims=True), ("dp", "mp"))
    weight = counts[None] * jnp.exp(scores - top)
    probs = weight / lax.psum(jnp.sum(weight, -1, keepdims=True), ("dp", "mp"))
    probs_low = probs.astype(BF16)
    z = mul("hcv,vi->hci", probs_low, hid)
    z = lax.psum_scatter(z, "mp", scatter_dimension=0, tiled=True)
    z = lax.psum_scatter(z, "dp", scatter_dimension=2, tiled=True).astype(BF16)
    att = lax.psum(mul("hci,ihk->hck", z, wv), "dp")
    att_low = att.astype(BF16)
    out = lax.psum(mul("hck,hke->ce", att_low, wo), "mp")
    first_sum = first_rows + lax.all_gather(out, "dp", axis=1, tiled=True)
    normed, normed_back = jax.vjp(layer_norm, first_sum, norms[2], norms[3])
    normed_mine = mine(normed).astype(BF16)
    inner = lax.psum(mul("ci,if->cf", normed_mine, wi), "dp")
    act, act_back = jax.vjp(partial(jax.nn.gelu, approximate=False), inner)
    act = act.astype(BF16)
    outer = lax.psum(mul("cf,fe->ce", act, wt), "mp")
    second_sum = normed + lax.all_gather(outer, "dp", axis=1, tiled=True)
    final, final_back = jax.vjp(layer_norm, second_sum, norms[4], norms[5])
    both = lax.all_gather(final, "enc", axis=0)
    loss, loss_back = jax.vjp(
        partial(
            contrast,
            negative_mask=slot_major(negative_mask),
            positive_index=slot_major(positive_index),
            used_rows=slot_major(used_rows),
        ),
        both[0],
        both[1, :blocks],
    )
    d_queries, d_passages = loss_back(jnp.ones((), F32))
    d_passages = jnp.concatenate([d_passages, jnp.zeros_like(d_passages)])
    d_final = jnp.where(is_query, d_queries, d_passages)
    d_second, d_gain2, d_shift2 = final_back(d_final)
    d_outer = mine(d_second).astype(BF16)
    g_outer = mul("cf,ce->fe", act, d_outer)
    d_act = lax.psum(mul("ce,fe->cf", d_outer, wt), "dp")
    d_inner = act_back(d_act)[0].astype(BF16)
    g_inner = mul("ci,cf->if", normed_mine, d_inner)
    d_in = lax.psum(mul("cf,if->ci", d_inner, wi), "mp")
    d_normed = d_second + lax.all_gather(d_in, "dp", axis=1, tiled=True)
    d_first, d_gain1, d_shift1 = normed_back(d_normed)
    d_attn = mine(d_first).astype(BF16)
    g_out = mul("hck,ce->hke", att_low, d_attn).reshape(w_out.shape[1:])
    d_att = lax.psum(mul("ce,hke->hck", d_attn, wo), "dp").astype(BF16)
    w = mul("hck,ihk->hci", d_att, wv).astype(BF16)
    mean_d = jnp.sum(att * d_att.astype(F32), -1, keepdims=True)
    w = lax.all_gather(lax.all_gather(w, "dp", axis=2, tiled=True), "mp", axis=0, tiled=True)
    mean_d = lax.all_gather(mean_d, "mp", axis=0, tiled=True)
    d_probs = mul("hci,vi->hcv", w, hid)
    d_scores = (probs * (d_probs - mean_d)).astype(BF16)
    y = mul("hcv,vi->hci", d_scores, hid)
    y = lax.psum_scatter(y, "mp", scatter_dimension=0, tiled=True)
    y = lax.psum_scatter(y, "dp", scatter_dimension=2, tiled=True).astype(BF16)
    dq = (lax.psum(mul("hci,ihk->hck", y, wk), "dp") * scale).astype(BF16)
    g_q = mul("ci,hck->ihk", first_mine, dq)
    g_k = mul("hci,hck->ihk", y, q) * scale
    g_v = mul("hci,hck->ihk", z, d_att)
    g_mixed = jnp.stack([g_q, g_k, g_v], 1).reshape(w_mixed.shape[1:])
    d_rows = lax.psum(mul("hck,ihk->ci", dq, wq), "mp")
    d_rows = (d_first + lax.all_gather(d_rows, "dp", axis=1, tiled=True)).astype(BF16)
    d_hidden = (
        mul("hcv,hci->vi", d_scores, u) * scale
        + mul("hcv,hci->vi", probs_low, w)
        + mul("cv,ci->vi", cls_hot.astype(BF16), d_rows)
    )
    g_table, d_gain0, d_shift0 = hidden_back(d_hidden)
    sums = lax.psum(jnp.stack([d_gain0, d_shift0]), ("dp", "mp"))
    g_norms = jnp.concatenate([sums, jnp.stack([d_gain1, d_shift1, d_gain2, d_shift2])])
    return (loss, (g_table, g_mixed, g_out, g_inner, g_outer, g_norms))


def on_device(
    token_ids,
    query_lengths,
    negative_mask,
    positive_index,
    used_rows,
    step_count,
    table,
    w_mixed,
    w_out,
    w_inner,
    w_outer,
    norm_params,
    table_m,
    table_v,
    mixed_m,
    mixed_v,
    out_m,
    out_v,
    inner_m,
    inner_v,
    outer_m,
    outer_v,
    norms_m,
    norms_v,
):
    loss, grads = gradients(
        token_ids,
        query_lengths,
        negative_mask,
        positive_index,
        used_rows,
        table,
        w_mixed,
        w_out,
        w_inner,
        w_outer,
        norm_params,
    )
    owner = (lax.axis_index("dp") == 0) & (lax.axis_index("mp") == 0)
    squares = jnp.where(owner, jnp.sum(grads[5] * grads[5]), 0.0)
    for grad in grads[:5]:
        squares = squares + jnp.sum(grad * grad)
    grad_norm = jnp.sqrt(lax.psum(squares, ("enc", "dp", "mp")))
    clip = jnp.minimum(1.0, clip_limit / (grad_norm + 1e-06))
    count = step_count[0].astype(F32)
    masters = (table, w_mixed, w_out, w_inner, w_outer, norm_params)
    firsts = (table_m, mixed_m, out_m, inner_m, outer_m, norms_m)
    seconds = (table_v, mixed_v, out_v, inner_v, outer_v, norms_v)
    results = [loss, grad_norm]
    for index in range(6):
        rate, decay = (0.5, 0.0) if index == 5 else (0.06, 0.01)
        results.extend(
            adam_step(
                masters[index],
                grads[index][None] * clip,
                firsts[index],
                seconds[index],
                rate,
                decay,
                count,
            )
        )
    return tuple(results)


def solution(mesh):
    table = P("enc", ("dp", "mp"), None)
    mixed = P("enc", "dp", None, "mp")
    columns = P("enc", "mp", "dp")
    units = P("enc", "dp", "mp")
    norms = P("enc", None, None)
    matrices = (table, mixed, columns, units, columns, norms)
    moments = tuple((spec for spec in matrices for _ in range(2)))
    updated = tuple((spec for spec in matrices for _ in range(3)))
    return jax.shard_map(
        on_device,
        mesh=mesh,
        in_specs=(P("enc", "dp", None), P("dp"), P(), P(), P(), P()) + matrices + moments,
        out_specs=(P(), P()) + updated,
        check_vma=False,
    )
```

profile of v0, /device:TPU:12, one launch (start us, length us, event | category | flops | bytes accessed | tf_op | source)
XLA Modules:
  0.0 815.6 jit_solution(12494069726686477999)
XLA Ops:
  13.8 13.3 %all-gather = s32[1,16,256]{2,0,1:T(1,128)S(1)} all-gather(s32[1,4,256]{2,0,1:T(1,128)S(1)} %copy.79), channel_id=2, replica_groups=mesh['enc'=2,'dp'=4,'mp'=4] {'dp'}, dimensions={1}, use_global_device_ids=true | all-gather | bytes 20480 | tf_op jit(solution)/shard_map/all_gather | solution.py:105
  40.0 8.2 %all-reduce.1 = s32[32]{0:T(128)S(1)} all-reduce(s32[32]{0:T(128)S(1)} %dynamic-update-slice), channel_id=1, replica_groups=mesh['enc'=2,'dp'=4,'mp'=4] {'dp'}, use_global_device_ids=true, to_apply=%add.1 | all-reduce | flops 32 | bytes 256
  51.7 86.6 %all-reduce.8.cloned.1.call-done = f32[32,768]{1,0:T(8,128)} async-done(((f32[32,768]{1,0:T(8,128)}), f32[32,768]{1,0:T(8,128)}) %all-reduce.8.cloned.1.call-update) | async-done | bytes 98320 | tf_op jit(solution)/shard_map/psum | solution.py:121
  139.3 14.6 %psum.99 = bf16[3,32,64]{2,1,0:T(8,128)(2,1)S(1)} all-reduce(f32[3,32,64]{2,1,0:T(8,128)S(1)} %convolution_bitcast_fusion.1), channel_id=1, replica_groups=mesh['enc'=2,'dp'=4,'mp'=4] {'dp'}, use_global_device_ids=true, to_apply=%region_3.4 | all-reduce | flops 6144 | bytes 36864 | tf_op jit(solution)/shard_map/psum | solution.py:125
  154.6 18.2 %all_gather.41 = bf16[3,32,768]{1,0,2:T(4,128)(2,1)S(1)} all-gather(bf16[3,32,192]{1,0,2:T(4,128)(2,1)S(1)} %copy.83), channel_id=1, replica_groups=mesh['enc'=2,'dp'=4,'mp'=4] {'dp'}, dimensions={2}, use_global_device_ids=true | all-gather | bytes 184320 | tf_op jit(solution)/shard_map/all_gather | solution.py:127
  173.3 10.2 %all_gather.42 = bf16[12,32,768]{2,1,0:T(8,128)(2,1)S(1)} all-gather(bf16[3,32,768]{2,1,0:T(8,128)(2,1)S(1)} %copy.84), channel_id=1, replica_groups=mesh['enc'=2,'dp'=4,'mp'=4] {'mp'}, dimensions={0}, use_global_device_ids=true | all-gather | bytes 737280 | tf_op jit(solution)/shard_map/all_gather | solution.py:127
  190.1 32.9 %pmax.7 = f32[12,32]{1,0:T(8,128)} all-reduce(f32[12,32]{1,0:T(8,128)} %get-tuple-element.83), channel_id=1, replica_groups=mesh['enc'=2,'dp'=4,'mp'=4] {'dp','mp'}, use_global_device_ids=true, to_apply=%region_5.6 | all-reduce | flops 384 | bytes 3072 | tf_op jit(solution)/shard_map/pmax | solution.py:129
  226.1 37.3 %psum.100 = f32[12,32]{1,0:T(8,128)} all-reduce(f32[12,32]{1,0:T(8,128)} %fusion.11), channel_id=1, replica_groups=mesh['enc'=2,'dp'=4,'mp'=4] {'dp','mp'}, use_global_device_ids=true, to_apply=%region_7.8 | all-reduce | flops 384 | bytes 3072 | tf_op jit(solution)/shard_map/psum | solution.py:131
  267.9 36.2 %reduce-scatter.17.cloned.1.call-done = f32[3,32,768]{2,1,0:T(8,128)} async-done(((f32[12,32,768]{2,1,0:T(8,128)}), f32[3,32,768]{2,1,0:T(8,128)}) %reduce-scatter.17.cloned.1.call-update) | async-done | bytes 294928
  311.7 13.1 %reduce-scatter.13.cloned.1.call-done = f32[192,96]{1,0:T(8,128)} async-done(((f32[768,96]{1,0:T(8,128)}), f32[192,96]{1,0:T(8,128)}) %reduce-scatter.13.cloned.1.call-update) | async-done | bytes 73744
  326.1 17.8 %psum.101 = f32[3,32,64]{2,1,0:T(8,128)S(1)} all-reduce(f32[3,32,64]{2,1,0:T(8,128)S(1)} %fusion.141), channel_id=1, replica_groups=mesh['enc'=2,'dp'=4,'mp'=4] {'dp'}, use_global_device_ids=true, to_apply=%region_10.11 | all-reduce | flops 6144 | bytes 49152 | tf_op jit(solution)/shard_map/psum | solution.py:136
  344.1 15.5 %psum.102 = f32[32,192]{1,0:T(8,128)S(1)} all-reduce(f32[32,192]{1,0:T(8,128)S(1)} %convolution_bitcast_fusion.3), channel_id=1, replica_groups=mesh['enc'=2,'dp'=4,'mp'=4] {'mp'}, use_global_device_ids=true, to_apply=%region_11.12 | all-reduce | flops 6144 | bytes 49152 | tf_op jit(solution)/shard_map/psum | solution.py:138
  359.5 13.5 %all-gather.3 = f32[4,192,32]{1,2,0:T(8,128)S(1)} all-gather(f32[1,192,32]{1,2,0:T(8,128)S(1)} %bitcast.263), channel_id=1, replica_groups=mesh['enc'=2,'dp'=4,'mp'=4] {'dp'}, dimensions={0}, use_global_device_ids=true | all-gather | bytes 122880 | tf_op jit(solution)/shard_map/all_gather | solution.py:139
  380.4 30.1 %all-reduce.10.cloned.1.call-done = f32[32,768]{1,0:T(8,128)} async-done(((f32[32,768]{1,0:T(8,128)}), f32[32,768]{1,0:T(8,128)}) %all-reduce.10.cloned.1.call-update) | async-done | bytes 98320 | tf_op jit(solution)/shard_map/psum | solution.py:142
  411.8 15.4 %psum.104 = f32[32,192]{1,0:T(8,128)S(1)} all-reduce(f32[32,192]{1,0:T(8,128)S(1)} %fusion.33), channel_id=1, replica_groups=mesh['enc'=2,'dp'=4,'mp'=4] {'mp'}, use_global_device_ids=true, to_apply=%region_15.16 | all-reduce | flops 6144 | bytes 49152 | tf_op jit(solution)/shard_map/psum | solution.py:145
  427.2 12.2 %all-gather.4 = f32[4,192,32]{1,2,0:T(8,128)S(1)} all-gather(f32[1,192,32]{1,2,0:T(8,128)S(1)} %bitcast.264), channel_id=1, replica_groups=mesh['enc'=2,'dp'=4,'mp'=4] {'dp'}, dimensions={0}, use_global_device_ids=true | all-gather | bytes 122880 | tf_op jit(solution)/shard_map/all_gather | solution.py:146
  449.2 33.5 %all-reduce.12.cloned.1.call-done = f32[32,768]{1,0:T(8,128)} async-done(((f32[32,768]{1,0:T(8,128)}), f32[32,768]{1,0:T(8,128)}) %all-reduce.12.cloned.1.call-update) | async-done | bytes 98320 | tf_op jit(solution)/shard_map/psum | solution.py:165
  483.9 15.4 %psum.106 = f32[32,192]{1,0:T(8,128)S(1)} all-reduce(f32[32,192]{1,0:T(8,128)S(1)} %fusion.35), channel_id=1, replica_groups=mesh['enc'=2,'dp'=4,'mp'=4] {'mp'}, use_global_device_ids=true, to_apply=%region_32.33 | all-reduce | flops 6144 | bytes 49152 | tf_op jit(solution)/shard_map/psum | solution.py:168
  499.3 12.2 %all-gather.5 = f32[4,192,32]{1,2,0:T(8,128)S(1)} all-gather(f32[1,192,32]{1,2,0:T(8,128)S(1)} %bitcast.265), channel_id=1, replica_groups=mesh['enc'=2,'dp'=4,'mp'=4] {'dp'}, dimensions={0}, use_global_device_ids=true | all-gather | bytes 122880 | tf_op jit(solution)/shard_map/all_gather | solution.py:169
  512.5 16.4 %psum.107 = bf16[3,32,64]{2,1,0:T(8,128)(2,1)S(1)} all-reduce(f32[3,32,64]{2,1,0:T(8,128)S(1)} %convolution_bitcast_fusion), channel_id=1, replica_groups=mesh['enc'=2,'dp'=4,'mp'=4] {'dp'}, use_global_device_ids=true, to_apply=%region_35.36 | all-reduce | flops 6144 | bytes 36864 | tf_op jit(solution)/shard_map/psum | solution.py:173
  529.3 15.9 %all_gather.48 = bf16[3,32,768]{1,0,2:T(4,128)(2,1)S(1)} all-gather(bf16[3,32,192]{1,0,2:T(4,128)(2,1)S(1)} %copy.91), channel_id=1, replica_groups=mesh['enc'=2,'dp'=4,'mp'=4] {'dp'}, dimensions={2}, use_global_device_ids=true | all-gather | bytes 184320 | tf_op jit(solution)/shard_map/all_gather | solution.py:176
  545.6 10.2 %all_gather.49 = bf16[12,32,768]{2,1,0:T(8,128)(2,1)S(1)} all-gather(bf16[3,32,768]{2,1,0:T(8,128)(2,1)S(1)} %copy.92), channel_id=1, replica_groups=mesh['enc'=2,'dp'=4,'mp'=4] {'mp'}, dimensions={0}, use_global_device_ids=true | all-gather | bytes 737280 | tf_op jit(solution)/shard_map/all_gather | solution.py:176
  555.9 7.1 all-gather.6
  587.9 13.2 %reduce-scatter.19.cloned.1.call-done = f32[3,32,768]{2,1,0:T(8,128)} async-done(((f32[12,32,768]{2,1,0:T(8,128)}), f32[3,32,768]{2,1,0:T(8,128)}) %reduce-scatter.19.cloned.1.call-update) | async-done | bytes 294928
  608.7 13.2 %reduce-scatter.15.cloned.1.call-done = f32[192,96]{1,0:T(8,128)} async-done(((f32[768,96]{1,0:T(8,128)}), f32[192,96]{1,0:T(8,128)}) %reduce-scatter.15.cloned.1.call-update) | async-done | bytes 73744
  624.2 17.8 %psum.108 = f32[3,32,64]{2,1,0:T(8,128)S(1)} all-reduce(f32[3,32,64]{2,1,0:T(8,128)S(1)} %fusion.139), channel_id=1, replica_groups=mesh['enc'=2,'dp'=4,'mp'=4] {'dp'}, use_global_device_ids=true, to_apply=%region_39.40 | all-reduce | flops 6144 | bytes 49152 | tf_op jit(solution)/shard_map/psum | solution.py:183
  643.1 15.4 %psum.109 = f32[32,192]{1,0:T(8,128)S(1)} all-reduce(f32[32,192]{1,0:T(8,128)S(1)} %convolution_bitcast_fusion.2), channel_id=1, replica_groups=mesh['enc'=2,'dp'=4,'mp'=4] {'mp'}, use_global_device_ids=true, to_apply=%region_40.41 | all-reduce | flops 6144 | bytes 49152 | tf_op jit(solution)/shard_map/psum | solution.py:188
  658.5 13.3 %all-gather.7 = f32[4,192,32]{1,2,0:T(8,128)S(1)} all-gather(f32[1,192,32]{1,2,0:T(8,128)S(1)} %bitcast.266), channel_id=1, replica_groups=mesh['enc'=2,'dp'=4,'mp'=4] {'dp'}, dimensions={0}, use_global_device_ids=true | all-gather | bytes 122880 | tf_op jit(solution)/shard_map/all_gather | solution.py:189
  672.0 12.5 %multiply_reduce_fusion.1 = (f32[1920]{0:T(1024)S(1)}, f32[768]{0:T(1024)S(1)}, f32[768]{0:T(1024)S(1)}, f32[1920,768]{1,0:T(8,128)}) fusion(f32[768]{0:T(1024)} %copy-done.40, f32[1920]{0:T(1024)S(1)} %broadcast_multiply_fusion.1, f32[1,1920,768]{2,1,0:T(8,128)} %param.30, f32[1920]{0:T(1024)S(1)} %fusion.93, f32[32,768]{1,0:T(8,128)} %copy-done.26, ...), kind=kOutput, calls=%fused_computation.11 | convolution fusion | flops 112173696 | bytes 23821952 | tf_op jit(solution)/shard_map/cv,ci->vi/dot_general | solution.py:27
  684.5 31.3 %psum.110 = f32[2,768]{1,0:T(2,128)S(1)} all-reduce(f32[2,768]{1,0:T(2,128)S(1)} %pad_maximum_fusion), channel_id=1, replica_groups=mesh['enc'=2,'dp'=4,'mp'=4] {'dp','mp'}, use_global_device_ids=true, to_apply=%region_43.44 | all-reduce | flops 1536 | bytes 12288 | tf_op jit(solution)/shard_map/psum | solution.py:196
  733.2 49.5 %psum.111 = f32[]{:T(128)} all-reduce(f32[]{:T(128)S(6)} %add.308), channel_id=1, replica_groups=mesh['enc'=2,'dp'=4,'mp'=4] {'enc','dp','mp'}, use_global_device_ids=true, to_apply=%region_56.57 | all-reduce | flops 1 | bytes 8 | tf_op jit(solution)/shard_map/psum | solution.py:244
  784.4 15.9 %multiply_subtract_fusion = (f32[1,1920,768]{2,1,0:T(8,128)}, f32[1,1920,768]{2,1,0:T(8,128)}, f32[1,1920,768]{2,1,0:T(8,128)}) fusion(f32[1,1920,768]{2,1,0:T(8,128)} %param.30, f32[]{:T(128)} %bitcast.52, f32[]{:T(128)} %bitcast.50, f32[]{:T(128)S(6)} %min.3, f32[1920,768]{1,0:T(8,128)} %copy-done.1, f32[1920]{0:T(1024)S(1)} %negate_multiply_fusion.1, ...), kind=kLoop, calls=%fused_computation.9 | loop fusion | flops 25067520 | bytes 41295372 | tf_op jit(solution)/shard_map/sub | solution.py:77
  (311 shorter events, 122.8 us)
Async XLA Ops:
  7.2 131.1 %all-reduce.8.cloned.1.call-start = ((), (), s32[]{:S(2)}) async-start(), calls=%async_computation.4 | async-start | bytes 196608 | tf_op jit(solution)/shard_map/psum | solution.py:121
  33.8 270.4 %reduce-scatter.17.cloned.1.call-start = ((), (), s32[]{:S(2)}) async-start(), calls=%async_computation.9 | async-start | bytes 1474560
  51.6 102.4 %copy-start.11 = (bf16[1,192,1,192]{1,3,2,0:T(8,128)(2,1)}, bf16[1,192,1,192]{1,3,2,0:T(8,128)(2,1)S(1)}, u32[]{:S(2)}) copy-start(bf16[1,192,1,192]{1,3,2,0:T(8,128)(2,1)S(1)} %copy.82) | copy-start | bytes 221188
  51.7 102.3 %copy-start.10 = (bf16[1,192,1,192]{1,3,2,0:T(8,128)(2,1)}, bf16[1,192,1,192]{1,3,2,0:T(8,128)(2,1)S(1)}, u32[]{:S(2)}) copy-start(bf16[1,192,1,192]{1,3,2,0:T(8,128)(2,1)S(1)} %copy.81) | copy-start | bytes 221188
  183.5 79.9 %copy-start.4 = (bf16[1920,768,1]{1,0,2:T(8,128)(2,1)S(1)}, bf16[1920,768,1]{1,0,2:T(8,128)(2,1)}, u32[]{:S(2)}) copy-start(bf16[1920,768,1]{1,0,2:T(8,128)(2,1)} %fusion.5) | copy-start | bytes 8847364
  267.9 107.4 %copy-start.2 = (f32[1,192,768]{2,1,0:T(8,128)S(1)}, f32[1,192,768]{2,1,0:T(8,128)}, u32[]{:S(2)}) copy-start(f32[1,192,768]{2,1,0:T(8,128)} %param.33) | copy-start | bytes 1769476
  267.9 143.8 %copy-start.3 = (f32[1,768,192]{1,2,0:T(8,128)S(1)}, f32[1,768,192]{1,2,0:T(8,128)}, u32[]{:S(2)}) copy-start(f32[1,768,192]{1,2,0:T(8,128)} %param.34) | copy-start | bytes 1769476
  267.9 56.9 %reduce-scatter.13.cloned.1.call-start = ((), (), s32[]{:S(2)}) async-start(), calls=%async_computation.7 | async-start | bytes 491520
  307.0 204.7 %copy-start.36 = (f32[768]{0:T(1024)S(1)}, f32[768]{0:T(1024)}, u32[]{:S(2)}) copy-start(f32[768]{0:T(1024)} %get-tuple-element.31) | copy-start | bytes 9220
  307.0 103.5 %all-reduce.10.cloned.1.call-start = ((), (), s32[]{:S(2)}) async-start(), calls=%async_computation.5 | async-start | bytes 196608 | tf_op jit(solution)/shard_map/psum | solution.py:142
  325.9 203.2 %copy-start.27 = (bf16[3,32,192]{2,1,0:T(8,128)(2,1)}, bf16[3,32,192]{2,1,0:T(8,128)(2,1)S(1)}, u32[]{:S(2)}) copy-start(bf16[3,32,192]{2,1,0:T(8,128)(2,1)S(1)} %copy.99) | copy-start | bytes 110596
  343.9 201.3 %copy-start.14 = (f32[3,32,64]{2,1,0:T(8,128)}, f32[3,32,64]{2,1,0:T(8,128)S(1)}, u32[]{:S(2)}) copy-start(f32[3,32,64]{2,1,0:T(8,128)S(1)} %psum.101) | copy-start | bytes 73732
  375.3 64.3 %copy-start.34 = (f32[32,768]{1,0:T(8,128)}, f32[32,768]{1,0:T(8,128)S(1)}, u32[]{:S(2)}) copy-start(f32[32,768]{1,0:T(8,128)S(1)} %multiply_add_fusion.4) | copy-start | bytes 294916
  376.2 186.8 %copy-start.9 = (f32[32,1920]{1,0:T(8,128)S(1)}, f32[32,1920]{1,0:T(8,128)}, u32[]{:S(2)}) copy-start(f32[32,1920]{1,0:T(8,128)} %get-tuple-element.75) | copy-start | bytes 737284
  376.2 106.5 %all-reduce.12.cloned.1.call-start = ((), (), s32[]{:S(2)}) async-start(), calls=%async_computation.6 | async-start | bytes 196608 | tf_op jit(solution)/shard_map/psum | solution.py:165
  447.5 64.0 %copy-start.35 = (f32[32,768]{1,0:T(8,128)}, f32[32,768]{1,0:T(8,128)S(1)}, u32[]{:S(2)}) copy-start(f32[32,768]{1,0:T(8,128)S(1)} %broadcast_add_fusion.1) | copy-start | bytes 294916
  448.4 152.7 %reduce-scatter.19.cloned.1.call-start = ((), (), s32[]{:S(2)}) async-start(), calls=%async_computation.10 | async-start | bytes 1474560
  483.7 83.7 %copy-start.29 = (bf16[32,768]{1,0:T(8,128)(2,1)}, bf16[32,768]{1,0:T(8,128)(2,1)S(1)}, u32[]{:S(2)}) copy-start(bf16[32,768]{1,0:T(8,128)(2,1)S(1)} %add_convert_fusion) | copy-start | bytes 147460
  512.0 64.4 %copy-start.48 = (f32[768]{0:T(1024)}, f32[768]{0:T(1024)S(1)}, u32[]{:S(2)}) copy-start(f32[768]{0:T(1024)S(1)} %get-tuple-element.25) | copy-start | bytes 9220
  512.0 64.9 %copy-start.46 = (f32[768]{0:T(1024)}, f32[768]{0:T(1024)S(1)}, u32[]{:S(2)}) copy-start(f32[768]{0:T(1024)S(1)} %get-tuple-element.28) | copy-start | bytes 9220
  512.3 55.1 %copy-start.26 = (f32[32,768]{1,0:T(8,128)}, f32[32,768]{1,0:T(8,128)S(1)}, u32[]{:S(2)}) copy-start(f32[32,768]{1,0:T(8,128)S(1)} %broadcast_add_fusion) | copy-start | bytes 294916
  571.0 50.9 %reduce-scatter.15.cloned.1.call-start = ((), (), s32[]{:S(2)}) async-start(), calls=%async_computation.8 | async-start | bytes 491520
  671.9 43.9 %copy-start.57 = (f32[1,768]{1,0:T(1,128)S(1)}, f32[1,768]{1,0:T(1,128)}, u32[]{:S(2)}) copy-start(f32[1,768]{1,0:T(1,128)} %reshape.653) | copy-start | bytes 9220
  672.0 43.9 %copy-start.58 = (f32[1,768]{1,0:T(1,128)S(1)}, f32[1,768]{1,0:T(1,128)}, u32[]{:S(2)}) copy-start(f32[1,768]{1,0:T(1,128)} %reshape.654) | copy-start | bytes 9220
  672.0 43.9 %copy-start.59 = (f32[1,768]{1,0:T(1,128)S(1)}, f32[1,768]{1,0:T(1,128)}, u32[]{:S(2)}) copy-start(f32[1,768]{1,0:T(1,128)} %reshape.651) | copy-start | bytes 9220
  672.0 43.9 %copy-start.60 = (f32[1,768]{1,0:T(1,128)S(1)}, f32[1,768]{1,0:T(1,128)}, u32[]{:S(2)}) copy-start(f32[1,768]{1,0:T(1,128)} %reshape.652) | copy-start | bytes 9220
  672.0 44.5 %copy-start.38 = (f32[1920]{0:T(1024)S(1)}, f32[1920]{0:T(1024)}, u32[]{:S(2)}) copy-start(f32[1920]{0:T(1024)} %copy-done.37) | copy-start | bytes 23044
  672.0 44.5 %copy-start.41 = (f32[768]{0:T(1024)S(1)}, f32[768]{0:T(1024)}, u32[]{:S(2)}) copy-start(f32[768]{0:T(1024)} %copy-done.40) | copy-start | bytes 9220
  722.7 60.9 %copy-start.49 = (f32[768]{0:T(1024)S(1)}, f32[768]{0:T(1024)}, u32[]{:S(2)}) copy-start(f32[768]{0:T(1024)} %copy-done.48) | copy-start | bytes 9220
  722.7 61.0 %copy-start.47 = (f32[768]{0:T(1024)S(1)}, f32[768]{0:T(1024)}, u32[]{:S(2)}) copy-start(f32[768]{0:T(1024)} %copy-done.46) | copy-start | bytes 9220
  722.7 61.0 %copy-start.45 = (f32[768]{0:T(1024)S(1)}, f32[768]{0:T(1024)}, u32[]{:S(2)}) copy-start(f32[768]{0:T(1024)} %get-tuple-element.23) | copy-start | bytes 9220
  722.7 61.0 %copy-start.43 = (f32[768]{0:T(1024)S(1)}, f32[768]{0:T(1024)}, u32[]{:S(2)}) copy-start(f32[768]{0:T(1024)} %get-tuple-element.27) | copy-start | bytes 9220
  (42 other events, 357.6 us)
Sparse Core Ops, SparseCore 0:
  33.9 104.3 all-reduce.7
  268.0 36.0 reduce-scatter.16
  307.2 17.5 reduce-scatter.12
  376.3 34.1 all-reduce.9
  448.5 34.1 all-reduce.11
  571.1 29.9 reduce-scatter.18
  604.2 17.6 reduce-scatter.14
where the time goes:
time: 817 us; the launch traced here: 816 us
  blocking collectives  416 us (51%)
  waiting for transfers between devices  226 us (28%)
  matrix products  62.6 us (8%)
  other arithmetic  59.2 us (7%)
  local copies, waits for them, and re-layouts  26.8 us (3%)
  between operations  24.9 us (3%)
    psum x1, waiting for transfers between devices, gradients(): lax.psum(jnp.dot(cls_hot.astype(F32), hidden, precision=exact_arithmetic_...  86.6 us
    unnamed x11, waiting for transfers between devices  75.8 us
    dot_general x26, matrix products, mul(): return jnp.einsum(spec, a, b, preferred_element_type=F32)  55.2 us
    psum x1, blocking collectives, on_device(): grad_norm = jnp.sqrt(lax.psum(squares, ('enc', 'dp', 'mp')))  49.5 us
    psum x1, blocking collectives, gradients(): probs = weight / lax.psum(jnp.sum(weight, -1, keepdims=True), ('dp', 'mp'))  37.3 us
    psum x1, waiting for transfers between devices, gradients(): d_act = lax.psum(mul('ce,fe->cf', d_outer, wt), 'dp')  33.5 us
    pmax x1, blocking collectives, gradients(): top = lax.pmax(jnp.max(scores, -1, keepdims=True), ('dp', 'mp'))  32.9 us
    psum x1, blocking collectives, gradients(): sums = lax.psum(jnp.stack([d_gain0, d_shift0]), ('dp', 'mp'))  31.3 us
  transfers between devices with their start and end apart: 7, of which 7 were waited for; matrix products, arithmetic and copies ran while one was open for 5% of the time, Pallas kernels for 0%

commit v1 on v0

--- a/solution.py
+++ b/solution.py
@@ -118,9 +118,8 @@
     embedded = lax.reduce_precision(table[0], 8, 7)
     hidden, hidden_back = jax.vjp(layer_norm, embedded, norms[0], norms[1])
     hid = hidden.astype(BF16)
-    first_rows = lax.psum(
-        jnp.dot(cls_hot.astype(F32), hidden, precision=exact_arithmetic_level), ("dp", "mp")
-    )
+    half = lax.psum(jnp.dot(cls_hot.astype(F32), hidden, precision=exact_arithmetic_level), "mp")
+    first_rows = lax.psum(half, "dp")
     first_mine = mine(first_rows).astype(BF16)
     q = lax.psum(mul("ci,ihk->hck", first_mine, wq), "dp").astype(BF16)
     u = mul("hck,ihk->hci", q, wk).astype(BF16)

time: 817 us -> 792 us (0.969)
  waiting for transfers between devices: 226 us -> 201 us
    psum x1, waiting for transfers between devices: 86.6 us -> 25.7 us  [gradients(): lax.psum(jnp.dot(cls_hot.astype(F32), hidden, precision=exact_arithmetic_...]
    psum x0 -> x1, waiting for transfers between devices: none -> 35.7 us  [gradients(): first_rows = lax.psum(half, 'dp')]
    unnamed x11 -> x12, waiting for transfers between devices: 75.8 us -> 75.6 us
  transfers between devices with their start and end apart: 7 -> 8, of which waited for: 7 -> 8; matrix products, arithmetic and copies ran while one was open for 5% -> 5% of each run, Pallas kernels for 0% -> 0%
where the time goes in v1:
time: 792 us; the launch traced here: 791 us
  blocking collectives  416 us (53%)
  waiting for transfers between devices  201 us (25%)
  matrix products  62.6 us (8%)
  other arithmetic  59.3 us (7%)
  local copies, waits for them, and re-layouts  26.8 us (3%)
  between operations  24.9 us (3%)
    unnamed x12, waiting for transfers between devices  75.6 us
    dot_general x26, matrix products, mul(): return jnp.einsum(spec, a, b, preferred_element_type=F32)  55.2 us
    psum x1, blocking collectives, on_device(): grad_norm = jnp.sqrt(lax.psum(squares, ('enc', 'dp', 'mp')))  49.4 us
    psum x1, blocking collectives, gradients(): probs = weight / lax.psum(jnp.sum(weight, -1, keepdims=True), ('dp', 'mp'))  37.4 us
    psum x1, waiting for transfers between devices, gradients(): first_rows = lax.psum(half, 'dp')  35.7 us
    psum x1, waiting for transfers between devices, gradients(): d_act = lax.psum(mul('ce,fe->cf', d_outer, wt), 'dp')  33.5 us
    pmax x1, blocking collectives, gradients(): top = lax.pmax(jnp.max(scores, -1, keepdims=True), ('dp', 'mp'))  33.3 us
    psum x1, blocking collectives, gradients(): sums = lax.psum(jnp.stack([d_gain0, d_shift0]), ('dp', 'mp'))  31.2 us
  transfers between devices with their start and end apart: 8, of which 8 were waited for; matrix products, arithmetic and copies ran while one was open for 5% of the time, Pallas kernels for 0%

profile of v1, /device:TPU:12, one launch (start us, length us, event | category | flops | bytes accessed | tf_op | source)
XLA Modules:
  0.0 790.5 jit_solution(5123507282730193173)
XLA Ops:
  13.8 13.3 %all-gather = s32[1,16,256]{2,0,1:T(1,128)S(1)} all-gather(s32[1,4,256]{2,0,1:T(1,128)S(1)} %copy.79), channel_id=2, replica_groups=mesh['enc'=2,'dp'=4,'mp'=4] {'dp'}, dimensions={1}, use_global_device_ids=true | all-gather | bytes 20480 | tf_op jit(solution)/shard_map/all_gather | solution.py:105
  40.0 8.2 %all-reduce.1 = s32[32]{0:T(128)S(1)} all-reduce(s32[32]{0:T(128)S(1)} %dynamic-update-slice), channel_id=1, replica_groups=mesh['enc'=2,'dp'=4,'mp'=4] {'dp'}, use_global_device_ids=true, to_apply=%add.1 | all-reduce | flops 32 | bytes 256
  50.9 25.7 %all-reduce.9.cloned.1.call-done = f32[32,768]{1,0:T(8,128)} async-done(((f32[32,768]{1,0:T(8,128)}), f32[32,768]{1,0:T(8,128)}) %all-reduce.9.cloned.1.call-update) | async-done | bytes 98320 | tf_op jit(solution)/shard_map/psum | solution.py:121
  77.6 35.7 %all-reduce.11.cloned.1.call-done = f32[32,768]{1,0:T(8,128)} async-done(((f32[32,768]{1,0:T(8,128)}), f32[32,768]{1,0:T(8,128)}) %all-reduce.11.cloned.1.call-update) | async-done | bytes 98320 | tf_op jit(solution)/shard_map/psum | solution.py:122
  114.2 14.9 %psum.107 = bf16[3,32,64]{2,1,0:T(8,128)(2,1)S(1)} all-reduce(f32[3,32,64]{2,1,0:T(8,128)S(1)} %convolution_bitcast_fusion.1), channel_id=1, replica_groups=mesh['enc'=2,'dp'=4,'mp'=4] {'dp'}, use_global_device_ids=true, to_apply=%region_4.5 | all-reduce | flops 6144 | bytes 36864 | tf_op jit(solution)/shard_map/psum | solution.py:124
  129.9 17.8 %all_gather.41 = bf16[3,32,768]{1,0,2:T(4,128)(2,1)S(1)} all-gather(bf16[3,32,192]{1,0,2:T(4,128)(2,1)S(1)} %copy.83), channel_id=1, replica_groups=mesh['enc'=2,'dp'=4,'mp'=4] {'dp'}, dimensions={2}, use_global_device_ids=true | all-gather | bytes 184320 | tf_op jit(solution)/shard_map/all_gather | solution.py:126
  148.1 10.3 %all_gather.42 = bf16[12,32,768]{2,1,0:T(8,128)(2,1)S(1)} all-gather(bf16[3,32,768]{2,1,0:T(8,128)(2,1)S(1)} %copy.84), channel_id=1, replica_groups=mesh['enc'=2,'dp'=4,'mp'=4] {'mp'}, dimensions={0}, use_global_device_ids=true | all-gather | bytes 737280 | tf_op jit(solution)/shard_map/all_gather | solution.py:126
  165.0 33.3 %pmax.7 = f32[12,32]{1,0:T(8,128)} all-reduce(f32[12,32]{1,0:T(8,128)} %get-tuple-element.83), channel_id=1, replica_groups=mesh['enc'=2,'dp'=4,'mp'=4] {'dp','mp'}, use_global_device_ids=true, to_apply=%region_6.7 | all-reduce | flops 384 | bytes 3072 | tf_op jit(solution)/shard_map/pmax | solution.py:128
  201.3 37.4 %psum.108 = f32[12,32]{1,0:T(8,128)} all-reduce(f32[12,32]{1,0:T(8,128)} %fusion.11), channel_id=1, replica_groups=mesh['enc'=2,'dp'=4,'mp'=4] {'dp','mp'}, use_global_device_ids=true, to_apply=%region_8.9 | all-reduce | flops 384 | bytes 3072 | tf_op jit(solution)/shard_map/psum | solution.py:130
  243.2 35.9 %reduce-scatter.17.cloned.1.call-done = f32[3,32,768]{2,1,0:T(8,128)} async-done(((f32[12,32,768]{2,1,0:T(8,128)}), f32[3,32,768]{2,1,0:T(8,128)}) %reduce-scatter.17.cloned.1.call-update) | async-done | bytes 294928
  286.6 13.1 %reduce-scatter.13.cloned.1.call-done = f32[192,96]{1,0:T(8,128)} async-done(((f32[768,96]{1,0:T(8,128)}), f32[192,96]{1,0:T(8,128)}) %reduce-scatter.13.cloned.1.call-update) | async-done | bytes 73744
  301.0 17.8 %psum.109 = f32[3,32,64]{2,1,0:T(8,128)S(1)} all-reduce(f32[3,32,64]{2,1,0:T(8,128)S(1)} %fusion.141), channel_id=1, replica_groups=mesh['enc'=2,'dp'=4,'mp'=4] {'dp'}, use_global_device_ids=true, to_apply=%region_11.12 | all-reduce | flops 6144 | bytes 49152 | tf_op jit(solution)/shard_map/psum | solution.py:135
  319.0 15.4 %psum.110 = f32[32,192]{1,0:T(8,128)S(1)} all-reduce(f32[32,192]{1,0:T(8,128)S(1)} %convolution_bitcast_fusion.3), channel_id=1, replica_groups=mesh['enc'=2,'dp'=4,'mp'=4] {'mp'}, use_global_device_ids=true, to_apply=%region_12.13 | all-reduce | flops 6144 | bytes 49152 | tf_op jit(solution)/shard_map/psum | solution.py:137
  334.5 13.5 %all-gather.3 = f32[4,192,32]{1,2,0:T(8,128)S(1)} all-gather(f32[1,192,32]{1,2,0:T(8,128)S(1)} %bitcast.263), channel_id=1, replica_groups=mesh['enc'=2,'dp'=4,'mp'=4] {'dp'}, dimensions={0}, use_global_device_ids=true | all-gather | bytes 122880 | tf_op jit(solution)/shard_map/all_gather | solution.py:138
  355.4 30.1 %all-reduce.13.cloned.1.call-done = f32[32,768]{1,0:T(8,128)} async-done(((f32[32,768]{1,0:T(8,128)}), f32[32,768]{1,0:T(8,128)}) %all-reduce.13.cloned.1.call-update) | async-done | bytes 98320 | tf_op jit(solution)/shard_map/psum | solution.py:141
  386.7 15.4 %psum.112 = f32[32,192]{1,0:T(8,128)S(1)} all-reduce(f32[32,192]{1,0:T(8,128)S(1)} %fusion.33), channel_id=1, replica_groups=mesh['enc'=2,'dp'=4,'mp'=4] {'mp'}, use_global_device_ids=true, to_apply=%region_16.17 | all-reduce | flops 6144 | bytes 49152 | tf_op jit(solution)/shard_map/psum | solution.py:144
  402.2 12.2 %all-gather.4 = f32[4,192,32]{1,2,0:T(8,128)S(1)} all-gather(f32[1,192,32]{1,2,0:T(8,128)S(1)} %bitcast.264), channel_id=1, replica_groups=mesh['enc'=2,'dp'=4,'mp'=4] {'dp'}, dimensions={0}, use_global_device_ids=true | all-gather | bytes 122880 | tf_op jit(solution)/shard_map/all_gather | solution.py:145
  424.1 33.5 %all-reduce.15.cloned.1.call-done = f32[32,768]{1,0:T(8,128)} async-done(((f32[32,768]{1,0:T(8,128)}), f32[32,768]{1,0:T(8,128)}) %all-reduce.15.cloned.1.call-update) | async-done | bytes 98320 | tf_op jit(solution)/shard_map/psum | solution.py:164
  458.8 15.4 %psum.114 = f32[32,192]{1,0:T(8,128)S(1)} all-reduce(f32[32,192]{1,0:T(8,128)S(1)} %fusion.35), channel_id=1, replica_groups=mesh['enc'=2,'dp'=4,'mp'=4] {'mp'}, use_global_device_ids=true, to_apply=%region_33.34 | all-reduce | flops 6144 | bytes 49152 | tf_op jit(solution)/shard_map/psum | solution.py:167
  474.2 12.2 %all-gather.5 = f32[4,192,32]{1,2,0:T(8,128)S(1)} all-gather(f32[1,192,32]{1,2,0:T(8,128)S(1)} %bitcast.265), channel_id=1, replica_groups=mesh['enc'=2,'dp'=4,'mp'=4] {'dp'}, dimensions={0}, use_global_device_ids=true | all-gather | bytes 122880 | tf_op jit(solution)/shard_map/all_gather | solution.py:168
  487.4 16.4 %psum.115 = bf16[3,32,64]{2,1,0:T(8,128)(2,1)S(1)} all-reduce(f32[3,32,64]{2,1,0:T(8,128)S(1)} %convolution_bitcast_fusion), channel_id=1, replica_groups=mesh['enc'=2,'dp'=4,'mp'=4] {'dp'}, use_global_device_ids=true, to_apply=%region_36.37 | all-reduce | flops 6144 | bytes 36864 | tf_op jit(solution)/shard_map/psum | solution.py:172
  504.2 15.9 %all_gather.48 = bf16[3,32,768]{1,0,2:T(4,128)(2,1)S(1)} all-gather(bf16[3,32,192]{1,0,2:T(4,128)(2,1)S(1)} %copy.91), channel_id=1, replica_groups=mesh['enc'=2,'dp'=4,'mp'=4] {'dp'}, dimensions={2}, use_global_device_ids=true | all-gather | bytes 184320 | tf_op jit(solution)/shard_map/all_gather | solution.py:175
  520.5 10.2 %all_gather.49 = bf16[12,32,768]{2,1,0:T(8,128)(2,1)S(1)} all-gather(bf16[3,32,768]{2,1,0:T(8,128)(2,1)S(1)} %copy.92), channel_id=1, replica_groups=mesh['enc'=2,'dp'=4,'mp'=4] {'mp'}, dimensions={0}, use_global_device_ids=true | all-gather | bytes 737280 | tf_op jit(solution)/shard_map/all_gather | solution.py:175
  562.8 13.3 %reduce-scatter.19.cloned.1.call-done = f32[3,32,768]{2,1,0:T(8,128)} async-done(((f32[12,32,768]{2,1,0:T(8,128)}), f32[3,32,768]{2,1,0:T(8,128)}) %reduce-scatter.19.cloned.1.call-update) | async-done | bytes 294928
  583.6 13.2 %reduce-scatter.15.cloned.1.call-done = f32[192,96]{1,0:T(8,128)} async-done(((f32[768,96]{1,0:T(8,128)}), f32[192,96]{1,0:T(8,128)}) %reduce-scatter.15.cloned.1.call-update) | async-done | bytes 73744
  599.2 17.8 %psum.116 = f32[3,32,64]{2,1,0:T(8,128)S(1)} all-reduce(f32[3,32,64]{2,1,0:T(8,128)S(1)} %fusion.139), channel_id=1, replica_groups=mesh['enc'=2,'dp'=4,'mp'=4] {'dp'}, use_global_device_ids=true, to_apply=%region_40.41 | all-reduce | flops 6144 | bytes 49152 | tf_op jit(solution)/shard_map/psum | solution.py:182
  618.0 15.4 %psum.117 = f32[32,192]{1,0:T(8,128)S(1)} all-reduce(f32[32,192]{1,0:T(8,128)S(1)} %convolution_bitcast_fusion.2), channel_id=1, replica_groups=mesh['enc'=2,'dp'=4,'mp'=4] {'mp'}, use_global_device_ids=true, to_apply=%region_41.42 | all-reduce | flops 6144 | bytes 49152 | tf_op jit(solution)/shard_map/psum | solution.py:187
  633.4 13.3 %all-gather.7 = f32[4,192,32]{1,2,0:T(8,128)S(1)} all-gather(f32[1,192,32]{1,2,0:T(8,128)S(1)} %bitcast.266), channel_id=1, replica_groups=mesh['enc'=2,'dp'=4,'mp'=4] {'dp'}, dimensions={0}, use_global_device_ids=true | all-gather | bytes 122880 | tf_op jit(solution)/shard_map/all_gather | solution.py:188
  647.0 12.5 %multiply_reduce_fusion.1 = (f32[1920]{0:T(1024)S(1)}, f32[768]{0:T(1024)S(1)}, f32[768]{0:T(1024)S(1)}, f32[1920,768]{1,0:T(8,128)}) fusion(f32[768]{0:T(1024)} %copy-done.40, f32[1920]{0:T(1024)S(1)} %broadcast_multiply_fusion.1, f32[1,1920,768]{2,1,0:T(8,128)} %param.30, f32[1920]{0:T(1024)S(1)} %fusion.93, f32[32,768]{1,0:T(8,128)} %copy-done.26, ...), kind=kOutput, calls=%fused_computation.11 | convolution fusion | flops 112173696 | bytes 23821952 | tf_op jit(solution)/shard_map/cv,ci->vi/dot_general | solution.py:27
  659.5 31.2 %psum.118 = f32[2,768]{1,0:T(2,128)S(1)} all-reduce(f32[2,768]{1,0:T(2,128)S(1)} %pad_maximum_fusion), channel_id=1, replica_groups=mesh['enc'=2,'dp'=4,'mp'=4] {'dp','mp'}, use_global_device_ids=true, to_apply=%region_44.45 | all-reduce | flops 1536 | bytes 12288 | tf_op jit(solution)/shard_map/psum | solution.py:195
  708.1 49.4 %psum.119 = f32[]{:T(128)} all-reduce(f32[]{:T(128)S(6)} %add.310), channel_id=1, replica_groups=mesh['enc'=2,'dp'=4,'mp'=4] {'enc','dp','mp'}, use_global_device_ids=true, to_apply=%region_57.58 | all-reduce | flops 1 | bytes 8 | tf_op jit(solution)/shard_map/psum | solution.py:243
  759.3 15.9 %multiply_subtract_fusion = (f32[1,1920,768]{2,1,0:T(8,128)}, f32[1,1920,768]{2,1,0:T(8,128)}, f32[1,1920,768]{2,1,0:T(8,128)}) fusion(f32[1,1920,768]{2,1,0:T(8,128)} %param.30, f32[]{:T(128)} %bitcast.52, f32[]{:T(128)} %bitcast.50, f32[]{:T(128)S(6)} %min.3, f32[1920,768]{1,0:T(8,128)} %copy-done.1, f32[1920]{0:T(1024)S(1)} %negate_multiply_fusion.1, ...), kind=kLoop, calls=%fused_computation.9 | loop fusion | flops 25067520 | bytes 41295372 | tf_op jit(solution)/shard_map/sub | solution.py:77
  (314 shorter events, 130.1 us)
Async XLA Ops:
  7.2 69.4 %all-reduce.9.cloned.1.call-start = ((), (), s32[]{:S(2)}) async-start(), calls=%async_computation.4 | async-start | bytes 196608 | tf_op jit(solution)/shard_map/psum | solution.py:121
  33.8 79.5 %all-reduce.11.cloned.1.call-start = ((), (), s32[]{:S(2)}) async-start(), calls=%async_computation.5 | async-start | bytes 196608 | tf_op jit(solution)/shard_map/psum | solution.py:122
  76.6 202.5 %reduce-scatter.17.cloned.1.call-start = ((), (), s32[]{:S(2)}) async-start(), calls=%async_computation.10 | async-start | bytes 1474560
  77.4 51.8 %copy-start.11 = (bf16[1,192,1,192]{1,3,2,0:T(8,128)(2,1)}, bf16[1,192,1,192]{1,3,2,0:T(8,128)(2,1)S(1)}, u32[]{:S(2)}) copy-start(bf16[1,192,1,192]{1,3,2,0:T(8,128)(2,1)S(1)} %copy.82) | copy-start | bytes 221188
  77.5 51.7 %copy-start.10 = (bf16[1,192,1,192]{1,3,2,0:T(8,128)(2,1)}, bf16[1,192,1,192]{1,3,2,0:T(8,128)(2,1)S(1)}, u32[]{:S(2)}) copy-start(bf16[1,192,1,192]{1,3,2,0:T(8,128)(2,1)S(1)} %copy.81) | copy-start | bytes 221188
  158.4 80.3 %copy-start.4 = (bf16[1920,768,1]{1,0,2:T(8,128)(2,1)S(1)}, bf16[1920,768,1]{1,0,2:T(8,128)(2,1)}, u32[]{:S(2)}) copy-start(bf16[1920,768,1]{1,0,2:T(8,128)(2,1)} %fusion.5) | copy-start | bytes 8847364
  243.1 107.1 %copy-start.2 = (f32[1,192,768]{2,1,0:T(8,128)S(1)}, f32[1,192,768]{2,1,0:T(8,128)}, u32[]{:S(2)}) copy-start(f32[1,192,768]{2,1,0:T(8,128)} %param.33) | copy-start | bytes 1769476
  243.1 143.4 %copy-start.3 = (f32[1,768,192]{1,2,0:T(8,128)S(1)}, f32[1,768,192]{1,2,0:T(8,128)}, u32[]{:S(2)}) copy-start(f32[1,768,192]{1,2,0:T(8,128)} %param.34) | copy-start | bytes 1769476
  243.1 56.6 %reduce-scatter.13.cloned.1.call-start = ((), (), s32[]{:S(2)}) async-start(), calls=%async_computation.8 | async-start | bytes 491520
  282.0 204.7 %copy-start.36 = (f32[768]{0:T(1024)S(1)}, f32[768]{0:T(1024)}, u32[]{:S(2)}) copy-start(f32[768]{0:T(1024)} %get-tuple-element.31) | copy-start | bytes 9220
  282.0 103.5 %all-reduce.13.cloned.1.call-start = ((), (), s32[]{:S(2)}) async-start(), calls=%async_computation.6 | async-start | bytes 196608 | tf_op jit(solution)/shard_map/psum | solution.py:141
  300.9 203.1 %copy-start.27 = (bf16[3,32,192]{2,1,0:T(8,128)(2,1)}, bf16[3,32,192]{2,1,0:T(8,128)(2,1)S(1)}, u32[]{:S(2)}) copy-start(bf16[3,32,192]{2,1,0:T(8,128)(2,1)S(1)} %copy.99) | copy-start | bytes 110596
  318.8 201.2 %copy-start.14 = (f32[3,32,64]{2,1,0:T(8,128)}, f32[3,32,64]{2,1,0:T(8,128)S(1)}, u32[]{:S(2)}) copy-start(f32[3,32,64]{2,1,0:T(8,128)S(1)} %psum.109) | copy-start | bytes 73732
  350.2 64.3 %copy-start.34 = (f32[32,768]{1,0:T(8,128)}, f32[32,768]{1,0:T(8,128)S(1)}, u32[]{:S(2)}) copy-start(f32[32,768]{1,0:T(8,128)S(1)} %multiply_add_fusion.4) | copy-start | bytes 294916
  351.1 186.8 %copy-start.9 = (f32[32,1920]{1,0:T(8,128)S(1)}, f32[32,1920]{1,0:T(8,128)}, u32[]{:S(2)}) copy-start(f32[32,1920]{1,0:T(8,128)} %get-tuple-element.75) | copy-start | bytes 737284
  351.1 106.5 %all-reduce.15.cloned.1.call-start = ((), (), s32[]{:S(2)}) async-start(), calls=%async_computation.7 | async-start | bytes 196608 | tf_op jit(solution)/shard_map/psum | solution.py:164
  422.4 64.0 %copy-start.35 = (f32[32,768]{1,0:T(8,128)}, f32[32,768]{1,0:T(8,128)S(1)}, u32[]{:S(2)}) copy-start(f32[32,768]{1,0:T(8,128)S(1)} %broadcast_add_fusion.1) | copy-start | bytes 294916
  423.3 152.8 %reduce-scatter.19.cloned.1.call-start = ((), (), s32[]{:S(2)}) async-start(), calls=%async_computation.11 | async-start | bytes 1474560
  458.6 83.7 %copy-start.29 = (bf16[32,768]{1,0:T(8,128)(2,1)}, bf16[32,768]{1,0:T(8,128)(2,1)S(1)}, u32[]{:S(2)}) copy-start(bf16[32,768]{1,0:T(8,128)(2,1)S(1)} %add_convert_fusion) | copy-start | bytes 147460
  486.9 64.4 %copy-start.48 = (f32[768]{0:T(1024)}, f32[768]{0:T(1024)S(1)}, u32[]{:S(2)}) copy-start(f32[768]{0:T(1024)S(1)} %get-tuple-element.25) | copy-start | bytes 9220
  486.9 64.9 %copy-start.46 = (f32[768]{0:T(1024)}, f32[768]{0:T(1024)S(1)}, u32[]{:S(2)}) copy-start(f32[768]{0:T(1024)S(1)} %get-tuple-element.28) | copy-start | bytes 9220
  487.2 55.1 %copy-start.26 = (f32[32,768]{1,0:T(8,128)}, f32[32,768]{1,0:T(8,128)S(1)}, u32[]{:S(2)}) copy-start(f32[32,768]{1,0:T(8,128)S(1)} %broadcast_add_fusion) | copy-start | bytes 294916
  545.9 50.9 %reduce-scatter.15.cloned.1.call-start = ((), (), s32[]{:S(2)}) async-start(), calls=%async_computation.9 | async-start | bytes 491520
  646.9 43.8 %copy-start.58 = (f32[1,768]{1,0:T(1,128)S(1)}, f32[1,768]{1,0:T(1,128)}, u32[]{:S(2)}) copy-start(f32[1,768]{1,0:T(1,128)} %reshape.654) | copy-start | bytes 9220
  646.9 43.8 %copy-start.59 = (f32[1,768]{1,0:T(1,128)S(1)}, f32[1,768]{1,0:T(1,128)}, u32[]{:S(2)}) copy-start(f32[1,768]{1,0:T(1,128)} %reshape.651) | copy-start | bytes 9220
  646.9 43.8 %copy-start.60 = (f32[1,768]{1,0:T(1,128)S(1)}, f32[1,768]{1,0:T(1,128)}, u32[]{:S(2)}) copy-start(f32[1,768]{1,0:T(1,128)} %reshape.652) | copy-start | bytes 9220
  647.0 44.4 %copy-start.38 = (f32[1920]{0:T(1024)S(1)}, f32[1920]{0:T(1024)}, u32[]{:S(2)}) copy-start(f32[1920]{0:T(1024)} %copy-done.37) | copy-start | bytes 23044
  647.0 44.4 %copy-start.41 = (f32[768]{0:T(1024)S(1)}, f32[768]{0:T(1024)}, u32[]{:S(2)}) copy-start(f32[768]{0:T(1024)} %copy-done.40) | copy-start | bytes 9220
  697.6 60.9 %copy-start.49 = (f32[768]{0:T(1024)S(1)}, f32[768]{0:T(1024)}, u32[]{:S(2)}) copy-start(f32[768]{0:T(1024)} %copy-done.48) | copy-start | bytes 9220
  697.6 60.9 %copy-start.47 = (f32[768]{0:T(1024)S(1)}, f32[768]{0:T(1024)}, u32[]{:S(2)}) copy-start(f32[768]{0:T(1024)} %copy-done.46) | copy-start | bytes 9220
  697.6 61.0 %copy-start.45 = (f32[768]{0:T(1024)S(1)}, f32[768]{0:T(1024)}, u32[]{:S(2)}) copy-start(f32[768]{0:T(1024)} %get-tuple-element.23) | copy-start | bytes 9220
  697.6 61.0 %copy-start.43 = (f32[768]{0:T(1024)S(1)}, f32[768]{0:T(1024)}, u32[]{:S(2)}) copy-start(f32[768]{0:T(1024)} %get-tuple-element.27) | copy-start | bytes 9220
  (43 other events, 409.4 us)
Sparse Core Ops, SparseCore 0:
  33.9 42.6 all-reduce.8
  79.0 34.2 all-reduce.10
  243.3 35.7 reduce-scatter.16
  282.1 17.5 reduce-scatter.12
  351.3 34.1 all-reduce.12
  423.4 34.1 all-reduce.14
  546.0 30.0 reduce-scatter.18
  579.1 17.6 reduce-scatter.14
